TPU v7x, 256 devices: a whole 4x4x8 slice. The times are simulated.
256 devices in a mesh: dp: 16 (over x, y_hi, core), expert: 16 (over z, y_lo).
Axes of the slice: x: 4, y: 4 (y_hi: 2, y_lo: 2; y = y_hi * 2 + y_lo), z: 8, core: 2. Of those that a mesh axis runs over, the one named last changes fastest.
Arguments:
- tokens: bfloat16 [2048, 4096], P('expert', 'dp'), may hold values from -6 to 6
- expert_ids: int32 [2048, 8], P('expert'), may hold values from 0 to 63, all different within a row; in each aligned block of 128 rows (0 to 127, 128 to 255, ...) at most 32 rows name the same one
- gate_prob: float32 [2048, 8], P('expert'), may hold values from 0.05 to 0.35
- w_gate: bfloat16 [64, 4096, 768], P('expert', 'dp'), may hold values from -0.09375 to 0.09375
- w_up: bfloat16 [64, 4096, 768], P('expert', 'dp'), may hold values from -0.09375 to 0.09375
- w_down: bfloat16 [64, 768, 4096], P('expert', None, 'dp'), may hold values from -0.21875 to 0.21875
- grad_out: bfloat16 [2048, 4096], P('expert', 'dp'), may hold values from -6 to 6
Outputs:
- mixed: bfloat16 [2048, 4096], P('expert', 'dp')
- grad_tokens: bfloat16 [2048, 4096], P('expert', 'dp')
- grad_gate: float32 [2048, 8], P('expert')
- grad_w_gate: bfloat16 [64, 4096, 768], P('expert', 'dp')
- grad_w_up: bfloat16 [64, 4096, 768], P('expert', 'dp')
- grad_w_down: bfloat16 [64, 768, 4096], P('expert', None, 'dp')
Inputs may be any that keep to these rules, and one draw needn't show every extreme that they name: `expert_ids`: each row names 8 different experts. Within the rows of one index of expert (aligned blocks of 128 rows) no expert is named by more than 32 rows, a bound that some block reaches.
All inputs are finite; a program needn't handle non-finite values.
Results may differ from a plain program's by a relative error of at most 0.035.
Values may be sent and summed in bfloat16 or wider, within the bound.
No kernel may reach another device: no remote copies, remote signals or barrier semaphores. Data moves between devices by JAX's collectives and lax.ppermute only.
A program may use at most 128 MiB of HBM per device.

v0:
```python
import jax
import jax.numpy as jnp
from jax import lax
from jax.sharding import PartitionSpec as P


def slot_tables(expert_ids, columns, per_device, capacity):
    flat_ids = expert_ids.reshape(-1)
    assign_count = flat_ids.shape[0]
    experts_all = columns * per_device
    onehot = (flat_ids[:, None] == jnp.arange(experts_all, dtype=jnp.int32)[None, :]).astype(
        jnp.int32
    )
    before = jnp.cumsum(onehot, axis=0) - onehot
    rank_in = jnp.sum(before * onehot, axis=1)
    slot_of = (flat_ids % per_device * columns + flat_ids // per_device) * capacity + rank_in
    slot_count = experts_all * capacity
    source = (
        jnp.full((slot_count,), assign_count, jnp.int32)
        .at[slot_of]
        .set(jnp.arange(assign_count, dtype=jnp.int32))
    )
    return (slot_of, source)


def run_groups(bundles, hidden_units):
    parties = lax.axis_size("dp")
    row_totals = [bundle[0].shape[0] * bundle[0].shape[1] for bundle in bundles]
    gate_part = jnp.concatenate(
        [
            jnp.einsum(
                "grd,gdf->grf", bundle[0], bundle[2], preferred_element_type=jnp.float32
            ).reshape(-1, hidden_units)
            for bundle in bundles
        ],
        axis=0,
    )
    up_part = jnp.concatenate(
        [
            jnp.einsum(
                "grd,gdf->grf", bundle[0], bundle[3], preferred_element_type=jnp.float32
            ).reshape(-1, hidden_units)
            for bundle in bundles
        ],
        axis=0,
    )
    total_rows = gate_part.shape[0]
    share_rows = total_rows // parties
    share_start = lax.axis_index("dp") * share_rows
    gate_pre, up_pre = (
        lax.psum(gate_part.astype(jnp.bfloat16), "dp").astype(jnp.float32),
        lax.psum(up_part.astype(jnp.bfloat16), "dp").astype(jnp.float32),
    )
    hidden = (jax.nn.silu(gate_pre) * up_pre).astype(jnp.bfloat16)
    gate_share = lax.dynamic_slice_in_dim(gate_pre, share_start, share_rows, 0)
    up_share = lax.dynamic_slice_in_dim(up_pre, share_start, share_rows, 0)
    hidden_part = jnp.concatenate(
        [
            jnp.einsum(
                "grd,gfd->grf", bundle[1], bundle[4], preferred_element_type=jnp.float32
            ).reshape(-1, hidden_units)
            for bundle in bundles
        ],
        axis=0,
    )
    hidden_grad = lax.psum_scatter(
        hidden_part.astype(jnp.bfloat16), "dp", scatter_dimension=0, tiled=True
    ).astype(jnp.float32)
    sigmoid_g = jax.nn.sigmoid(gate_share)
    gate_grad = (
        hidden_grad * up_share * sigmoid_g * (1.0 + gate_share * (1.0 - sigmoid_g))
    ).astype(jnp.bfloat16)
    up_grad = (hidden_grad * gate_share * sigmoid_g).astype(jnp.bfloat16)
    gate_rows, up_rows = (
        lax.all_gather(gate_grad, "dp", axis=0, tiled=True),
        lax.all_gather(up_grad, "dp", axis=0, tiled=True),
    )
    outputs = []
    offset = 0
    for bundle, row_total in zip(bundles, row_totals):
        piece_shape = (bundle[0].shape[0], bundle[0].shape[1], hidden_units)
        hidden_piece = hidden.reshape(piece_shape)
        gate_piece = gate_rows.reshape(piece_shape)
        up_piece = up_rows.reshape(piece_shape)
        offset = offset + row_total
        expert_out = jnp.einsum(
            "grf,gfd->grd", hidden_piece, bundle[4], preferred_element_type=jnp.float32
        ).astype(jnp.bfloat16)
        slot_grad = (
            jnp.einsum("grf,gdf->grd", gate_piece, bundle[2], preferred_element_type=jnp.float32)
            + jnp.einsum("grf,gdf->grd", up_piece, bundle[3], preferred_element_type=jnp.float32)
        ).astype(jnp.bfloat16)
        dw_gate = jnp.einsum(
            "grd,grf->gdf", bundle[0], gate_piece, preferred_element_type=jnp.float32
        )
        dw_up = jnp.einsum("grd,grf->gdf", bundle[0], up_piece, preferred_element_type=jnp.float32)
        dw_down = jnp.einsum(
            "grf,grd->gfd", hidden_piece, bundle[1], preferred_element_type=jnp.float32
        )
        outputs.append((expert_out, slot_grad, dw_gate, dw_up, dw_down))
    return outputs


def on_device(tokens, expert_ids, gate_prob, w_gate, w_up, w_down, grad_out):
    tok_rows, fanout = expert_ids.shape
    per_device, slice_width, hidden_units = w_gate.shape
    columns = lax.axis_size("expert")
    capacity = 2 * tok_rows * fanout // (per_device * columns)
    slot_count = per_device * columns * capacity
    assign_count = tok_rows * fanout
    slot_of, source = slot_tables(expert_ids, columns, per_device, capacity)
    filled = source < assign_count
    safe_src = jnp.minimum(source, assign_count - 1)
    tok_index = safe_src // fanout
    gate_flat = gate_prob.reshape(-1)
    token_buffer = jnp.where(filled[:, None], tokens[tok_index], jnp.zeros((), jnp.bfloat16))
    gate_slots = jnp.where(filled, gate_flat[safe_src], jnp.zeros((), jnp.float32))
    grad_buffer = (gate_slots[:, None] * grad_out[tok_index].astype(jnp.float32)).astype(
        jnp.bfloat16
    )
    layout = (per_device, columns, capacity, slice_width)
    sent_tokens, sent_grads = (
        lax.all_to_all(
            token_buffer.reshape(layout), "expert", split_axis=1, concat_axis=1, tiled=True
        ),
        lax.all_to_all(
            grad_buffer.reshape(layout), "expert", split_axis=1, concat_axis=1, tiled=True
        ),
    )
    bundles = [
        (
            sent_tokens.reshape(per_device, columns * capacity, slice_width),
            sent_grads.reshape(per_device, columns * capacity, slice_width),
            w_gate,
            w_up,
            w_down,
        )
    ]
    results = run_groups(bundles, hidden_units)
    expert_out = results[0][0].reshape(layout)
    slot_grad = results[0][1].reshape(layout)
    total_gate = results[0][2]
    total_up = results[0][3]
    total_down = results[0][4]
    grad_w_gate = total_gate.astype(jnp.bfloat16)
    grad_w_up = total_up.astype(jnp.bfloat16)
    grad_w_down = total_down.astype(jnp.bfloat16)
    back_out, back_grad = (
        lax.all_to_all(expert_out, "expert", split_axis=1, concat_axis=1, tiled=True),
        lax.all_to_all(slot_grad, "expert", split_axis=1, concat_axis=1, tiled=True),
    )
    out_rows = (
        back_out.reshape(slot_count, slice_width)[slot_of]
        .reshape(tok_rows, fanout, slice_width)
        .astype(jnp.float32)
    )
    grad_rows = (
        back_grad.reshape(slot_count, slice_width)[slot_of]
        .reshape(tok_rows, fanout, slice_width)
        .astype(jnp.float32)
    )
    mixed = jnp.sum(gate_prob[:, :, None] * out_rows, axis=1).astype(jnp.bfloat16)
    grad_tokens = jnp.sum(grad_rows, axis=1).astype(jnp.bfloat16)
    partial_dots = jnp.sum(out_rows * grad_out.astype(jnp.float32)[:, None, :], axis=2)
    grad_gate = lax.psum(partial_dots, "dp")
    return (mixed, grad_tokens, grad_gate, grad_w_gate, grad_w_up, grad_w_down)


def solution(mesh):
    return jax.shard_map(
        on_device,
        mesh=mesh,
        in_specs=(
            P("expert", "dp"),
            P("expert", None),
            P("expert", None),
            P("expert", "dp", None),
            P("expert", "dp", None),
            P("expert", None, "dp"),
            P("expert", "dp"),
        ),
        out_specs=(
            P("expert", "dp"),
            P("expert", "dp"),
            P("expert", None),
            P("expert", "dp", None),
            P("expert", "dp", None),
            P("expert", None, "dp"),
        ),
        check_vma=False,
    )
```

profile of v0, /device:TPU:32, one launch (start us, length us, event | category | flops | bytes accessed | tf_op | source)
XLA Modules:
  0.0 592.9 jit_solution(16468973395299543634)
XLA Ops:
  9.3 18.0 %reduce-window.6 = s32[64,8,128]{2,1,0:T(8,128)S(1)} reduce-window(s32[64,8,128]{2,1,0:T(8,128)S(1)} %fusion.11, s32[]{:T(128)} %constant.58.clone.1), window={size=1x1x128 pad=0_0x0_0x127_0}, to_apply=%region_0.0 | reduce-window | flops 8323072 | bytes 524292 | tf_op jit(solution)/shard_map/reduce-window
  28.0 4.3 scatter_custom_fusion
  32.4 8.6 %gather_fusion.2 = f32[2048]{0:T(1024)S(1)} fusion(f32[1024]{0:T(1024)S(1)} %reshape.230, s32[2048]{0:T(1024)S(1)} %get-tuple-element.26), kind=kCustom, calls=%fused_computation.2 | custom fusion | bytes 24576 | tf_op jit(solution)/shard_map/gather | solution.py:117
  41.1 7.5 %gather_fusion = bf16[2048,256]{1,0:T(8,128)(2,1)S(1)} fusion(bf16[128,256]{1,0:T(8,128)(2,1)S(1)} %copy-done.2, s32[2048]{0:T(1024)S(1)} %get-tuple-element.27), kind=kCustom, calls=%fused_computation | custom fusion | bytes 2105344 | tf_op jit(solution)/shard_map/gather | solution.py:116
  49.1 35.7 %all_to_all.20 = bf16[4,16,32,256]{3,2,0,1:T(8,128)(2,1)S(1)} all-to-all(bf16[4,16,32,256]{3,2,0,1:T(8,128)(2,1)S(1)} %copy_select_fusion), channel_id=1, replica_groups=mesh['dp'=16,'expert'=16] {'expert'}, dimensions={1} | all-to-all | bytes 2097152 | tf_op jit(solution)/shard_map/all_to_all | solution.py:123
  91.0 7.5 %gather_fusion.3 = bf16[2048,256]{1,0:T(8,128)(2,1)S(1)} fusion(bf16[128,256]{1,0:T(8,128)(2,1)S(1)} %copy-done.1, s32[2048]{0:T(1024)S(1)} %get-tuple-element.27), kind=kCustom, calls=%fused_computation.3 | custom fusion | bytes 2105344 | tf_op jit(solution)/shard_map/gather | solution.py:118
  98.8 32.5 %all_to_all.21 = bf16[4,16,32,256]{3,2,0,1:T(8,128)(2,1)S(1)} all-to-all(bf16[4,16,32,256]{3,2,0,1:T(8,128)(2,1)S(1)} %fusion), channel_id=1, replica_groups=mesh['dp'=16,'expert'=16] {'expert'}, dimensions={1} | all-to-all | bytes 2097152 | tf_op jit(solution)/shard_map/all_to_all | solution.py:126
  131.4 2.7 convolution_convert_fusion
  134.2 139.9 %all-reduce.3.cloned.1.call-done = (bf16[2048,768]{1,0:T(8,128)(2,1)}, bf16[2048,768]{1,0:T(8,128)(2,1)}) async-done(((bf16[2048,768]{1,0:T(8,128)(2,1)}, bf16[2048,768]{1,0:T(8,128)(2,1)}), (bf16[2048,768]{1,0:T(8,128)(2,1)}, bf16[2048,768]{1,0:T(8,128)(2,1)})) %all-reduce.3.cloned.1.call-update) | async-done | bytes 6291472 | tf_op jit(solution)/shard_map/psum | solution.py:52
  274.1 5.2 convert_element_type.91
  279.3 3.1 convert_element_type.94
  282.4 79.0 %reduce-scatter.2.cloned.1.call-done = bf16[128,768]{1,0:T(8,128)(2,1)} async-done(((bf16[2048,768]{1,0:T(8,128)(2,1)}), bf16[128,768]{1,0:T(8,128)(2,1)}) %reduce-scatter.2.cloned.1.call-update) | async-done | bytes 196624 | tf_op jit(solution)/shard_map/reduce_scatter | solution.py:66
  364.2 3.8 multiply_convert_fusion
  370.8 7.5 %all-to-all-start.1 = ((bf16[4,16,32,256]{3,2,0,1:T(8,128)(2,1)}), bf16[4,16,32,256]{3,2,0,1:T(8,128)(2,1)}, u32[]{:S(2)}, u32[]{:S(2)}) async-start(bf16[4,16,32,256]{3,2,0,1:T(8,128)(2,1)} %copy.55), calls=%async_computation.1 | async-start | bytes 2097152 | tf_op jit(solution)/shard_map/all_to_all | solution.py:149
  378.3 42.8 %all-gather.3.cloned.1.call-done = bf16[2048,768]{1,0:T(8,128)(2,1)} async-done(((bf16[128,768]{1,0:T(8,128)(2,1)}), bf16[2048,768]{1,0:T(8,128)(2,1)}) %all-gather.3.cloned.1.call-update) | async-done | bytes 3145744 | tf_op jit(solution)/shard_map/all_gather | solution.py:75
  421.1 4.7 fusion.20
  425.8 54.7 %all-gather.5.cloned.1.call-done = bf16[2048,768]{1,0:T(8,128)(2,1)} async-done(((bf16[128,768]{1,0:T(8,128)(2,1)}), bf16[2048,768]{1,0:T(8,128)(2,1)}) %all-gather.5.cloned.1.call-update) | async-done | bytes 3145744 | tf_op jit(solution)/shard_map/all_gather | solution.py:76
  480.5 4.0 add_convert_fusion
  485.6 7.5 %all-to-all-start.3 = ((bf16[4,16,32,256]{3,2,0,1:T(8,128)(2,1)}), bf16[4,16,32,256]{3,2,0,1:T(8,128)(2,1)}, u32[]{:S(2)}, u32[]{:S(2)}) async-start(bf16[4,16,32,256]{3,2,0,1:T(8,128)(2,1)} %copy.61), calls=%async_computation.4 | async-start | bytes 2097152 | tf_op jit(solution)/shard_map/all_to_all | solution.py:150
  493.1 4.3 convolution_convert_fusion.3
  498.7 3.9 gather_fusion.1
  503.8 69.0 %psum.23 = f32[128,8]{1,0:T(8,128)S(1)} all-reduce(f32[128,8]{1,0:T(8,128)S(1)} %get-tuple-element.18), channel_id=1, replica_groups=mesh['dp'=16,'expert'=16] {'dp'}, use_global_device_ids=true, to_apply=%region_10.11 | all-reduce | flops 1024 | bytes 8192 | tf_op jit(solution)/shard_map/psum | solution.py:165
  573.4 4.5 convolution_convert_fusion.5
  581.5 3.9 gather_fusion.4
  (70 shorter events, 24.1 us)
Async XLA Ops:
  7.2 124.3 %copy-start = (bf16[4,768,256]{2,1,0:T(8,128)(2,1)S(1)}, bf16[4,768,256]{2,1,0:T(8,128)(2,1)}, u32[]{:S(2)}) copy-start(bf16[4,768,256]{2,1,0:T(8,128)(2,1)} %param.12) | copy-start | bytes 4718596
  7.2 266.9 %all-reduce.3.cloned.1.call-start = ((), (), s32[]{:S(2)}) async-start(), calls=%async_computation.8 | async-start | bytes 12582912 | tf_op jit(solution)/shard_map/psum | solution.py:52
  32.4 8.7 %copy-start.2 = (bf16[128,256]{1,0:T(8,128)(2,1)S(1)}, bf16[128,256]{1,0:T(8,128)(2,1)}, u32[]{:S(2)}) copy-start(bf16[128,256]{1,0:T(8,128)(2,1)} %param.7) | copy-start | bytes 196612
  48.6 36.3 %copy-start.9 = (bf16[4,256,768]{2,1,0:T(8,128)(2,1)S(1)}, bf16[4,256,768]{2,1,0:T(8,128)(2,1)}, u32[]{:S(2)}) copy-start(bf16[4,256,768]{2,1,0:T(8,128)(2,1)} %param.11) | copy-start | bytes 4718596
  84.8 5.3 copy-start.3
  84.8 2.7 copy-start.8
  90.2 0.8 copy-start.1
  90.2 271.3 %reduce-scatter.2.cloned.1.call-start = ((), (), s32[]{:S(2)}) async-start(), calls=%async_computation.5 | async-start | bytes 3342336 | tf_op jit(solution)/shard_map/reduce_scatter | solution.py:66
  134.2 287.0 %all-gather.3.cloned.1.call-start = ((), (), s32[]{:S(2)}) async-start(), calls=%async_computation.6 | async-start | bytes 3342336 | tf_op jit(solution)/shard_map/all_gather | solution.py:75
  274.1 5.2 copy-start.5
  363.6 116.8 %all-gather.5.cloned.1.call-start = ((), (), s32[]{:S(2)}) async-start(), calls=%async_computation.7 | async-start | bytes 3342336 | tf_op jit(solution)/shard_map/all_gather | solution.py:76
  368.1 1.7 copy-start.7
  370.8 114.8 %all-to-all-start.1 = ((bf16[4,16,32,256]{3,2,0,1:T(8,128)(2,1)}), bf16[4,16,32,256]{3,2,0,1:T(8,128)(2,1)}, u32[]{:S(2)}, u32[]{:S(2)}) async-start(bf16[4,16,32,256]{3,2,0,1:T(8,128)(2,1)} %copy.55), calls=%async_computation.1 | async-start | bytes 2097152 | tf_op jit(solution)/shard_map/all_to_all | solution.py:149
  485.6 94.6 %all-to-all-start.3 = ((bf16[4,16,32,256]{3,2,0,1:T(8,128)(2,1)}), bf16[4,16,32,256]{3,2,0,1:T(8,128)(2,1)}, u32[]{:S(2)}, u32[]{:S(2)}) async-start(bf16[4,16,32,256]{3,2,0,1:T(8,128)(2,1)} %copy.61), calls=%async_computation.4 | async-start | bytes 2097152 | tf_op jit(solution)/shard_map/all_to_all | solution.py:150
  503.8 74.2 %copy-start.4 = (bf16[4,16,32,256]{3,2,1,0:T(8,128)(2,1)S(1)}, bf16[4,16,32,256]{3,2,1,0:T(8,128)(2,1)}, u32[]{:S(2)}) copy-start(bf16[4,16,32,256]{3,2,1,0:T(8,128)(2,1)} %copy-done.3) | copy-start | bytes 3145732
  573.4 4.5 copy-start.6
Sparse Core Ops, SparseCore 0:
  90.3 183.7 all-reduce.2
  278.4 83.0 reduce-scatter.1
  364.2 56.9 all-gather.2
  424.2 56.2 all-gather.4
where the time goes:
time: 594 us; the launch traced here: 593 us
  waiting for transfers between devices  317 us (53%)
  blocking collectives  137 us (23%)
  local copies, waits for them, and re-layouts  45.3 us (8%)
  other arithmetic  35.5 us (6%)
  matrix products  28.7 us (5%)
  starting transfers between devices  15.2 us (3%)
  between operations  14.1 us (2%)
    psum x1, waiting for transfers between devices, run_groups(): lax.psum(up_part.astype(jnp.bfloat16), 'dp').astype(jnp.float32)  140 us
    reduce_scatter x1, waiting for transfers between devices, run_groups(): lax.psum_scatter(hidden_part.astype(jnp.bfloat16), 'dp', scatter_dimensio...  79 us
    psum x1, blocking collectives, on_device(): grad_gate = lax.psum(partial_dots, 'dp')  69 us
    all_gather x1, waiting for transfers between devices, run_groups(): lax.all_gather(up_grad, 'dp', axis=0, tiled=True)  54.7 us
    all_gather x1, waiting for transfers between devices, run_groups(): lax.all_gather(gate_grad, 'dp', axis=0, tiled=True)  42.8 us
    all_to_all x1, blocking collectives, on_device(): lax.all_to_all(token_buffer.reshape(layout), 'expert', split_axis=1, conc...  35.7 us
    all_to_all x1, blocking collectives, on_device(): lax.all_to_all(grad_buffer.reshape(layout), 'expert', split_axis=1, conca...  32.5 us
    another operation x3, other arithmetic  18.2 us
  transfers between devices with their start and end apart: 6, of which 4 were waited for; matrix products, arithmetic and copies ran while one was open for 9% of the time, Pallas kernels for 0%

commit v1 on v0

--- a/solution.py
+++ b/solution.py
@@ -2,6 +2,7 @@
 import jax.numpy as jnp
 from jax import lax
 from jax.sharding import PartitionSpec as P
+from jax.lax import all_gather
 
 
 def slot_tables(expert_ids, columns, per_device, capacity):
@@ -49,7 +50,7 @@
     share_start = lax.axis_index("dp") * share_rows
     gate_pre, up_pre = (
         lax.psum(gate_part.astype(jnp.bfloat16), "dp").astype(jnp.float32),
-        lax.psum(up_part.astype(jnp.bfloat16), "dp").astype(jnp.float32),
+        all_gather(up_part.astype(jnp.bfloat16), "dp").sum(axis=0).astype(jnp.float32),
     )
     hidden = (jax.nn.silu(gate_pre) * up_pre).astype(jnp.bfloat16)
     gate_share = lax.dynamic_slice_in_dim(gate_pre, share_start, share_rows, 0)

time: 594 us -> 836 us (1.41)
  waiting for transfers between devices: 317 us -> 539 us
  other arithmetic: 35.5 us -> 56.5 us
    all_gather x0 -> x1, waiting for transfers between devices: none -> 269 us  [run_groups(): all_gather(up_part.astype(jnp.bfloat16), 'dp').sum(axis=0)]
    psum x1, waiting for transfers between devices: 140 us -> 112 us  [run_groups(): lax.psum(gate_part.astype(jnp.bfloat16), 'dp').astype(jnp.float32)]
    reduce_sum x0 -> x1, other arithmetic: none -> 19.1 us  [run_groups(): all_gather(up_part.astype(jnp.bfloat16), 'dp').sum(axis=0)]
    reduce_scatter x1, waiting for transfers between devices: 79 us -> 60.4 us  [run_groups(): lax.psum_scatter(hidden_part.astype(jnp.bfloat16), 'dp', scatter_dimensio...]
  transfers between devices with their start and end apart: 6 -> 7, of which waited for: 4 -> 5; matrix products, arithmetic and copies ran while one was open for 9% -> 9% of each run, Pallas kernels for 0% -> 0%
where the time goes in v1:
time: 836 us
  waiting for transfers between devices  539 us (64%)
  blocking collectives  136 us (16%)
  other arithmetic  56.5 us (7%)
  local copies, waits for them, and re-layouts  44.7 us (5%)
  matrix products  30 us (4%)
  starting transfers between devices  15.2 us (2%)
  between operations  14.1 us (2%)
    all_gather x1, waiting for transfers between devices, run_groups(): all_gather(up_part.astype(jnp.bfloat16), 'dp').sum(axis=0)  269 us
    psum x1, waiting for transfers between devices, run_groups(): lax.psum(gate_part.astype(jnp.bfloat16), 'dp').astype(jnp.float32)  112 us
    psum x1, blocking collectives, on_device(): grad_gate = lax.psum(partial_dots, 'dp')  69 us
    reduce_scatter x1, waiting for transfers between devices, run_groups(): lax.psum_scatter(hidden_part.astype(jnp.bfloat16), 'dp', scatter_dimensio...  60.4 us
    all_gather x1, waiting for transfers between devices, run_groups(): lax.all_gather(up_grad, 'dp', axis=0, tiled=True)  54.7 us
    all_gather x1, waiting for transfers between devices, run_groups(): lax.all_gather(gate_grad, 'dp', axis=0, tiled=True)  42.5 us
    all_to_all x1, blocking collectives, on_device(): lax.all_to_all(token_buffer.reshape(layout), 'expert', split_axis=1, conc...  35.7 us
    all_to_all x1, blocking collectives, on_device(): lax.all_to_all(grad_buffer.reshape(layout), 'expert', split_axis=1, conca...  31.4 us
  transfers between devices with their start and end apart: 7, of which 5 were waited for; matrix products, arithmetic and copies ran while one was open for 9% of the time, Pallas kernels for 0%

profile of v1, /device:TPU:32, one launch (start us, length us, event | category | flops | bytes accessed | tf_op | source)
XLA Modules:
  0.0 835.6 jit_solution(2381519533392355521)
XLA Ops:
  8.4 18.0 %reduce-window.6 = s32[64,8,128]{2,1,0:T(8,128)S(1)} reduce-window(s32[64,8,128]{2,1,0:T(8,128)S(1)} %fusion.11, s32[]{:T(128)} %constant.59.clone.1), window={size=1x1x128 pad=0_0x0_0x127_0}, to_apply=%region_0.0 | reduce-window | flops 8323072 | bytes 524292 | tf_op jit(solution)/shard_map/reduce-window
  27.1 4.3 scatter_custom_fusion
  32.4 8.6 %gather_fusion.2 = f32[2048]{0:T(1024)S(1)} fusion(f32[1024]{0:T(1024)S(1)} %reshape.240, s32[2048]{0:T(1024)S(1)} %get-tuple-element.24), kind=kCustom, calls=%fused_computation.2 | custom fusion | bytes 24576 | tf_op jit(solution)/shard_map/gather | solution.py:118
  41.1 7.5 gather_fusion
  49.1 35.7 %all_to_all.20 = bf16[4,16,32,256]{3,2,0,1:T(8,128)(2,1)S(1)} all-to-all(bf16[4,16,32,256]{3,2,0,1:T(8,128)(2,1)S(1)} %copy_select_fusion), channel_id=1, replica_groups=mesh['dp'=16,'expert'=16] {'expert'}, dimensions={1} | all-to-all | bytes 2097152 | tf_op jit(solution)/shard_map/all_to_all | solution.py:124
  87.6 4.0 convolution_convert_fusion.1
  91.7 7.5 gather_fusion.3
  99.6 31.4 %all_to_all.21 = bf16[4,16,32,256]{3,2,0,1:T(8,128)(2,1)S(1)} all-to-all(bf16[4,16,32,256]{3,2,0,1:T(8,128)(2,1)S(1)} %fusion), channel_id=1, replica_groups=mesh['dp'=16,'expert'=16] {'expert'}, dimensions={1} | all-to-all | bytes 2097152 | tf_op jit(solution)/shard_map/all_to_all | solution.py:127
  133.9 112.0 %all-reduce.2.cloned.1.call-done = bf16[2048,768]{1,0:T(8,128)(2,1)} async-done(((bf16[2048,768]{1,0:T(8,128)(2,1)}), bf16[2048,768]{1,0:T(8,128)(2,1)}) %all-reduce.2.cloned.1.call-update) | async-done | bytes 3145744 | tf_op jit(solution)/shard_map/psum | solution.py:52
  245.8 5.0 convert_element_type.100
  250.8 268.9 %all-gather.4.cloned.1.call-done = bf16[16,2048,768]{2,1,0:T(8,128)(2,1)} async-done(((bf16[1,2048,768]{2,1,0:T(8,128)(2,1)}), bf16[16,2048,768]{2,1,0:T(8,128)(2,1)}) %all-gather.4.cloned.1.call-update) | async-done | bytes 50331664 | tf_op jit(solution)/shard_map/all_gather | solution.py:53
  519.7 19.1 %reduce_sum.55 = bf16[2048,768]{1,0:T(8,128)(2,1)} reduce(bf16[16,2048,768]{2,1,0:T(8,128)(2,1)} %all-gather.4.cloned.1.call-done, bf16[]{:T(256)} %constant.71.clone.1), dimensions={0}, to_apply=%region_5.6 | reduce | flops 23592960 | bytes 53477376 | tf_op jit(solution)/shard_map/reduce_sum | solution.py:53
  538.8 5.2 convert_element_type.103
  544.0 60.4 %reduce-scatter.2.cloned.1.call-done = bf16[128,768]{1,0:T(8,128)(2,1)} async-done(((bf16[2048,768]{1,0:T(8,128)(2,1)}), bf16[128,768]{1,0:T(8,128)(2,1)}) %reduce-scatter.2.cloned.1.call-update) | async-done | bytes 196624 | tf_op jit(solution)/shard_map/reduce_scatter | solution.py:67
  613.7 7.5 all-to-all-start.1
  621.3 42.5 %all-gather.6.cloned.1.call-done = bf16[2048,768]{1,0:T(8,128)(2,1)} async-done(((bf16[128,768]{1,0:T(8,128)(2,1)}), bf16[2048,768]{1,0:T(8,128)(2,1)}) %all-gather.6.cloned.1.call-update) | async-done | bytes 3145744 | tf_op jit(solution)/shard_map/all_gather | solution.py:76
  663.8 4.7 fusion.20
  668.5 54.7 %all-gather.8.cloned.1.call-done = bf16[2048,768]{1,0:T(8,128)(2,1)} async-done(((bf16[128,768]{1,0:T(8,128)(2,1)}), bf16[2048,768]{1,0:T(8,128)(2,1)}) %all-gather.8.cloned.1.call-update) | async-done | bytes 3145744 | tf_op jit(solution)/shard_map/all_gather | solution.py:77
  723.2 4.0 add_convert_fusion
  728.3 7.5 all-to-all-start.3
  735.8 4.3 convolution_convert_fusion.3
  741.4 3.9 gather_fusion.1
  746.5 69.0 %psum.15 = f32[128,8]{1,0:T(8,128)S(1)} all-reduce(f32[128,8]{1,0:T(8,128)S(1)} %get-tuple-element.18), channel_id=1, replica_groups=mesh['dp'=16,'expert'=16] {'dp'}, use_global_device_ids=true, to_apply=%region_10.11 | all-reduce | flops 1024 | bytes 8192 | tf_op jit(solution)/shard_map/psum | solution.py:166
  816.1 4.5 convolution_convert_fusion.4
  (70 shorter events, 31.3 us)
Async XLA Ops:
  7.2 123.9 %copy-start = (bf16[4,768,256]{2,1,0:T(8,128)(2,1)S(1)}, bf16[4,768,256]{2,1,0:T(8,128)(2,1)}, u32[]{:S(2)}) copy-start(bf16[4,768,256]{2,1,0:T(8,128)(2,1)} %param.12) | copy-start | bytes 4718596
  7.2 238.6 %all-reduce.2.cloned.1.call-start = ((), (), s32[]{:S(2)}) async-start(), calls=%async_computation.5 | async-start | bytes 6291456 | tf_op jit(solution)/shard_map/psum | solution.py:52
  32.4 8.7 %copy-start.2 = (bf16[128,256]{1,0:T(8,128)(2,1)S(1)}, bf16[128,256]{1,0:T(8,128)(2,1)}, u32[]{:S(2)}) copy-start(bf16[128,256]{1,0:T(8,128)(2,1)} %param.7) | copy-start | bytes 196612
  48.6 36.2 %copy-start.7 = (bf16[4,256,768]{2,1,0:T(8,128)(2,1)S(1)}, bf16[4,256,768]{2,1,0:T(8,128)(2,1)}, u32[]{:S(2)}) copy-start(bf16[4,256,768]{2,1,0:T(8,128)(2,1)} %param.10) | copy-start | bytes 4718596
  84.8 2.7 copy-start.3
  87.5 4.2 copy-start.1
  87.5 432.2 %all-gather.4.cloned.1.call-start = ((), (), s32[]{:S(2)}) async-start(), calls=%async_computation.6 | async-start | bytes 53477376 | tf_op jit(solution)/shard_map/all_gather | solution.py:53
  91.6 512.8 %reduce-scatter.2.cloned.1.call-start = ((), (), s32[]{:S(2)}) async-start(), calls=%async_computation.7 | async-start | bytes 3342336 | tf_op jit(solution)/shard_map/reduce_scatter | solution.py:67
  133.8 530.0 %all-gather.6.cloned.1.call-start = ((), (), s32[]{:S(2)}) async-start(), calls=%async_computation.8 | async-start | bytes 3342336 | tf_op jit(solution)/shard_map/all_gather | solution.py:76
  606.6 116.6 %all-gather.8.cloned.1.call-start = ((), (), s32[]{:S(2)}) async-start(), calls=%async_computation.9 | async-start | bytes 3342336 | tf_op jit(solution)/shard_map/all_gather | solution.py:77
  611.0 1.7 copy-start.6
  613.7 114.5 %all-to-all-start.1 = ((bf16[4,16,32,256]{3,2,0,1:T(8,128)(2,1)}), bf16[4,16,32,256]{3,2,0,1:T(8,128)(2,1)}, u32[]{:S(2)}, u32[]{:S(2)}) async-start(bf16[4,16,32,256]{3,2,0,1:T(8,128)(2,1)} %copy.55), calls=%async_computation.1 | async-start | bytes 2097152 | tf_op jit(solution)/shard_map/all_to_all | solution.py:150
  728.3 94.6 %all-to-all-start.3 = ((bf16[4,16,32,256]{3,2,0,1:T(8,128)(2,1)}), bf16[4,16,32,256]{3,2,0,1:T(8,128)(2,1)}, u32[]{:S(2)}, u32[]{:S(2)}) async-start(bf16[4,16,32,256]{3,2,0,1:T(8,128)(2,1)} %copy.61), calls=%async_computation.4 | async-start | bytes 2097152 | tf_op jit(solution)/shard_map/all_to_all | solution.py:151
  746.5 74.1 %copy-start.4 = (bf16[4,16,32,256]{3,2,1,0:T(8,128)(2,1)S(1)}, bf16[4,16,32,256]{3,2,1,0:T(8,128)(2,1)}, u32[]{:S(2)}) copy-start(bf16[4,16,32,256]{3,2,1,0:T(8,128)(2,1)} %copy-done.3) | copy-start | bytes 3145732
  816.1 4.5 copy-start.5
Sparse Core Ops, SparseCore 0:
  87.6 158.1 all-reduce.1
  248.5 271.1 all-gather.3
  524.0 80.3 reduce-scatter.1
  607.0 56.7 all-gather.5
  666.9 56.2 all-gather.7
